TPU v7x, 512 devices: a whole 4x4x16 slice. The times are simulated.
512 devices in a mesh: dom: 64 (over z, y), src: 4 (over x), rel: 2 (over core).
Axes of the slice: x: 4, y: 4, z: 16, core: 2. Of those that a mesh axis runs over, the one named last changes fastest.
Arguments:
- source_feats: bfloat16 [131072, 256], P(('dom', 'src', 'rel')), may hold values from -6 to 6
- rel_weight: bfloat16 [12, 256, 256], P('rel'), may hold values from -0.375 to 0.375
- halo_pick: int32 [64, 4, 2, 64], P('dom', 'src', 'rel'), may hold values from 0 to 1
- entry_index: int32 [64, 4, 2, 3, 64], P('dom', 'src', 'rel'), may hold values from 0 to 63, as said below
- entry_count: int32 [64, 4, 2], P('dom', 'src', 'rel'), may hold values from 1 to 64, as said below
- entry_values: bfloat16 [64, 4, 2, 64, 128, 128], P('dom', 'src', 'rel'), may hold values from -0.125 to 0.125
- cotangent: bfloat16 [131072, 256], P(('dom', 'src', 'rel')), may hold values from -0.0546875 to 0.0546875
Outputs:
- out_feats: bfloat16 [131072, 256], P(('dom', 'src', 'rel'))
- grad_rel: float32 [12, 256, 256], P('rel')
Inputs may be any that keep to these rules, and one draw needn't show every extreme that they name: `entry_index`: row 0 of an entry is a target block below 16, row 1 a partition below 64, row 2 a relation below 6. Over all 64 entries of one (p,s,g), every partition is named 64 // 64 times or once more. `entry_count`: live entries come first; some (p,s,g) has all 64 entries live in every draw.
All inputs are finite; a program needn't handle non-finite values.
Results may differ from a plain program's by a relative error of at most 0.0057.
Values may be sent and summed in bfloat16 or wider, within the bound.
A program may use at most 64 MiB of HBM per device.

v0:
```python
import jax
import jax.numpy as jnp
from jax import lax
from jax.sharding import PartitionSpec as P


def silu_slope(pre_values):
    logistic = jax.nn.sigmoid(pre_values)
    return logistic * (1.0 + pre_values * (1.0 - logistic))


def local(source_feats, rel_weight, halo_pick, entry_index, entry_count, entry_values, cotangent):
    partitions = lax.axis_size("dom")
    tile_rows = entry_values.shape[-1]
    features = source_feats.shape[1]
    chosen = halo_pick.reshape(-1)
    everyone = lax.all_gather(source_feats, "dom", axis=0, tiled=True)
    everyone = everyone.reshape(partitions, -1, tile_rows, features)
    halo_blocks = everyone[jnp.arange(partitions, dtype=jnp.int32), chosen]
    own_rows = cotangent.shape[0]
    tgt_blocks = own_rows * lax.axis_size("src") * lax.axis_size("rel") // tile_rows
    rel_local = rel_weight.shape[0]
    entry_table = entry_index.reshape(3, -1)
    slot_total = entry_table.shape[1]
    values = entry_values.reshape(-1, tile_rows, tile_rows)
    picked = halo_blocks[entry_table[1]]
    messages = jnp.einsum("eij,ejd->eid", values, picked, preferred_element_type=jnp.float32)
    live_mask = jnp.arange(slot_total, dtype=jnp.int32) < entry_count.reshape(())
    target_slot = entry_table[2] * tgt_blocks + entry_table[0]
    slot_numbers = jnp.arange(rel_local * tgt_blocks, dtype=jnp.int32)
    placement = ((slot_numbers[:, None] == target_slot[None, :]) & live_mask[None, :]).astype(
        jnp.float32
    )
    totals = jnp.einsum(
        "se,eid->sid",
        placement,
        messages,
        precision=lax.Precision.HIGHEST,
        preferred_element_type=jnp.float32,
    )
    relation_terms = totals.astype(jnp.bfloat16).reshape(
        rel_local, tgt_blocks * tile_rows, features
    )
    summed = lax.psum_scatter(
        jnp.einsum("rtd,rde->te", relation_terms, rel_weight, preferred_element_type=jnp.float32),
        ("src", "rel"),
        scatter_dimension=0,
        tiled=True,
    )
    out_feats = jax.nn.silu(summed).astype(jnp.bfloat16)
    local_grad = (cotangent.astype(jnp.float32) * silu_slope(summed)).astype(jnp.bfloat16)
    grad_rows = lax.all_gather(local_grad, ("src", "rel"), axis=0, tiled=True)
    weight_terms = jnp.einsum(
        "rtd,te->rde", relation_terms, grad_rows, preferred_element_type=jnp.float32
    )
    grad_rel = lax.psum(weight_terms, ("dom", "src"))
    return (out_feats, grad_rel)


def solution(mesh):
    return jax.shard_map(
        local,
        mesh=mesh,
        in_specs=(
            P(("dom", "src", "rel"), None),
            P("rel", None, None),
            P("dom", "src", "rel", None),
            P("dom", "src", "rel", None, None),
            P("dom", "src", "rel"),
            P("dom", "src", "rel", None, None, None),
            P(("dom", "src", "rel"), None),
        ),
        out_specs=(P(("dom", "src", "rel"), None), P("rel", None, None)),
        check_vma=False,
    )
```

profile of v0, /device:TPU:2, one launch (start us, length us, event | category | flops | bytes accessed | tf_op | source)
XLA Modules:
  0.0 711.4 jit_solution(15321850771566686382)
XLA Ops:
  7.2 0.0 copy-start
  7.2 0.0 all-gather.3.cloned.1.call-start
  7.2 0.7 all-gather.3.cloned.1.call-update
  7.9 0.0 reduce-scatter.2.cloned.1.call-start
  8.6 0.7 fusion.17
  9.3 0.7 add_bitcast_fusion
  10.0 0.7 fusion.18
  10.6 160.9 %all-gather.3.cloned.1.call-done = bf16[16384,256]{1,0:T(8,128)(2,1)} async-done(((bf16[256,256]{1,0:T(8,128)(2,1)}), bf16[16384,256]{1,0:T(8,128)(2,1)}) %all-gather.3.cloned.1.call-update) | async-done | bytes 8388624 | tf_op jit(solution)/shard_map/all_gather | solution.py:17
  171.5 6.2 gather_fusion
  177.7 4.9 gather_fusion.1
  182.6 0.0 copy-done
  182.6 6.7 fusion.5
  189.3 9.2 %copy.12 = f32[64,256,128]{1,0,2:T(8,128)} copy(f32[64,256,128]{2,1,0:T(8,128)} %fusion.5) | data formatting | bytes 16777216 | tf_op jit(solution)/shard_map/eij,ejd->eid/dot_general | solution.py:27
  198.5 8.4 %fusion.2 = bf16[96,128,256]{2,0,1:T(8,128)(2,1)S(1)} fusion(f32[64,256,128]{1,0,2:T(8,128)} %copy.12, s32[64]{0:T(128)S(1)} %add_bitcast_fusion, pred[64]{0:T(512)(128)(4,1)S(1)} %iota_compare_fusion.1), kind=kOutput, calls=%fused_computation.4 | convolution fusion | flops 2419077120 | bytes 14680384 | tf_op jit(solution)/shard_map/se,eid->sid/dot_general | solution.py:34
  207.0 0.0 copy-start.3
  207.0 3.7 copy.10
  210.6 0.0 copy-start.1
  210.6 2.6 copy-done.1
  213.3 0.0 copy-done.3
  213.3 3.3 convolution_bitcast_fusion
  216.5 0.0 reduce-scatter.2.cloned.1.call-update
  216.6 0.0 all-gather.5.cloned.1.call-start
  216.6 33.4 %reduce-scatter.2.cloned.1.call-done = f32[256,256]{1,0:T(8,128)} async-done(((f32[2048,256]{1,0:T(8,128)}), f32[256,256]{1,0:T(8,128)}) %reduce-scatter.2.cloned.1.call-update) | async-done | bytes 262160 | tf_op jit(solution)/shard_map/reduce_scatter | solution.py:44
  250.0 0.0 copy-done.2
  250.0 1.8 multiply_convert_fusion
  251.7 0.0 all-gather.5.cloned.1.call-update
  251.8 0.0 all-reduce.2.cloned.1.call-start
  251.8 32.6 %all-gather.5.cloned.1.call-done = bf16[2048,256]{1,0:T(8,128)(2,1)} async-done(((bf16[256,256]{1,0:T(8,128)(2,1)}), bf16[2048,256]{1,0:T(8,128)(2,1)}) %all-gather.5.cloned.1.call-update) | async-done | bytes 1048592 | tf_op jit(solution)/shard_map/all_gather | solution.py:52
  284.4 6.0 fusion.7
  290.4 0.0 all-reduce.2.cloned.1.call-update
  290.4 411.6 %all-reduce.2.cloned.1.call-done = f32[6,256,256]{2,1,0:T(8,128)} async-done(((f32[6,256,256]{2,1,0:T(8,128)}), f32[6,256,256]{2,1,0:T(8,128)}) %all-reduce.2.cloned.1.call-update) | async-done | bytes 1572880 | tf_op jit(solution)/shard_map/psum | solution.py:56
  702.1 2.7 copy.16
  (3 shorter events, 0.0 us)
Async XLA Ops:
  7.2 175.5 %copy-start = (bf16[1,1,1,64,128,128]{5,4,3,2,1,0:T(8,128)(2,1)S(1)}, bf16[1,1,1,64,128,128]{5,4,3,2,1,0:T(8,128)(2,1)}, u32[]{:S(2)}) copy-start(bf16[1,1,1,64,128,128]{5,4,3,2,1,0:T(8,128)(2,1)} %param.12) | copy-start | bytes 6291460
  7.2 164.4 %all-gather.3.cloned.1.call-start = ((), (), s32[]{:S(2)}) async-start(), calls=%async_computation.1 | async-start | bytes 8519680 | tf_op jit(solution)/shard_map/all_gather | solution.py:17
  7.9 242.1 %reduce-scatter.2.cloned.1.call-start = ((), (), s32[]{:S(2)}) async-start(), calls=%async_computation.2 | async-start | bytes 2359296 | tf_op jit(solution)/shard_map/reduce_scatter | solution.py:44
  207.0 6.3 copy-start.3
  210.6 2.7 copy-start.1
  213.3 36.7 %copy-start.2 = (bf16[256,256]{1,0:T(8,128)(2,1)S(1)}, bf16[256,256]{1,0:T(8,128)(2,1)}, u32[]{:S(2)}) copy-start(bf16[256,256]{1,0:T(8,128)(2,1)} %param.13) | copy-start | bytes 393220
  216.6 67.8 %all-gather.5.cloned.1.call-start = ((), (), s32[]{:S(2)}) async-start(), calls=%async_computation.3 | async-start | bytes 1179648 | tf_op jit(solution)/shard_map/all_gather | solution.py:52
  251.8 450.3 %all-reduce.2.cloned.1.call-start = ((), (), s32[]{:S(2)}) async-start(), calls=%async_computation.4 | async-start | bytes 3145728 | tf_op jit(solution)/shard_map/psum | solution.py:56
Sparse Core Ops, SparseCore 0:
  10.9 160.5 all-gather.2
  216.7 33.2 reduce-scatter.1
  252.7 31.6 all-gather.4
  290.6 411.4 all-reduce.1
where the time goes:
time: 712 us; the launch traced here: 711 us
  waiting for transfers between devices  639 us (90%)
  local copies, waits for them, and re-layouts  29.3 us (4%)
  matrix products  24.4 us (3%)
  between operations  14.5 us (2%)
    psum x1, waiting for transfers between devices, local(): grad_rel = lax.psum(weight_terms, ('dom', 'src'))  412 us
    all_gather x1, waiting for transfers between devices, local(): everyone = lax.all_gather(source_feats, 'dom', axis=0, tiled=True)  161 us
    reduce_scatter x1, waiting for transfers between devices, local(): lax.psum_scatter(jnp.einsum('rtd,rde->te', relation_terms, rel_weight, pr...  33.4 us
    all_gather x1, waiting for transfers between devices, local(): grad_rows = lax.all_gather(local_grad, ('src', 'rel'), axis=0, tiled=True)  32.6 us
  transfers between devices with their start and end apart: 4, of which 4 were waited for; matrix products, arithmetic and copies ran while one was open for 0% of the time, Pallas kernels for 0%

commit v1 on v0

--- a/solution.py
+++ b/solution.py
@@ -53,7 +53,7 @@
     weight_terms = jnp.einsum(
         "rtd,te->rde", relation_terms, grad_rows, preferred_element_type=jnp.float32
     )
-    grad_rel = lax.psum(weight_terms, ("dom", "src"))
+    grad_rel = jax.lax.psum(jax.lax.psum(weight_terms, axis_name="dom"), axis_name="src")
     return (out_feats, grad_rel)
 
 

time: 712 us -> 645 us (0.906)
  the two profiles are of different devices: /device:TPU:2 before, /device:TPU:1 now
where the time goes in v1:
time: 645 us; the launch traced here: 644 us
  waiting for transfers between devices  572 us (89%)
  local copies, waits for them, and re-layouts  29.3 us (5%)
  matrix products  24.4 us (4%)
  between operations  14.5 us (2%)
    psum x1, waiting for transfers between devices, local(): jax.lax.psum(weight_terms, axis_name='dom')  269 us
    all_gather x1, waiting for transfers between devices, local(): everyone = lax.all_gather(source_feats, 'dom', axis=0, tiled=True)  154 us
    psum x1, waiting for transfers between devices, local(): jax.lax.psum(jax.lax.psum(weight_terms, axis_name='dom'), axis_name='src')  72.8 us
    reduce_scatter x1, waiting for transfers between devices, local(): lax.psum_scatter(jnp.einsum('rtd,rde->te', relation_terms, rel_weight, pr...  42.6 us
    all_gather x1, waiting for transfers between devices, local(): grad_rows = lax.all_gather(local_grad, ('src', 'rel'), axis=0, tiled=True)  32.9 us
  transfers between devices with their start and end apart: 5, of which 5 were waited for; matrix products, arithmetic and copies ran while one was open for 0% of the time, Pallas kernels for 0%

profile of v1, /device:TPU:1, one launch (start us, length us, event | category | flops | bytes accessed | tf_op | source)
XLA Modules:
  0.0 644.1 jit_solution(10540853925808808199)
XLA Ops:
  7.2 0.0 copy-start
  7.2 0.0 all-gather.3.cloned.1.call-start
  7.2 0.7 all-gather.3.cloned.1.call-update
  7.9 0.0 reduce-scatter.2.cloned.1.call-start
  8.6 0.7 fusion.17
  9.3 0.7 add_bitcast_fusion
  10.0 0.7 fusion.18
  10.6 154.0 %all-gather.3.cloned.1.call-done = bf16[16384,256]{1,0:T(8,128)(2,1)} async-done(((bf16[256,256]{1,0:T(8,128)(2,1)}), bf16[16384,256]{1,0:T(8,128)(2,1)}) %all-gather.3.cloned.1.call-update) | async-done | bytes 8388624 | tf_op jit(solution)/shard_map/all_gather | solution.py:17
  164.6 6.2 gather_fusion
  170.8 4.9 gather_fusion.1
  175.7 6.7 %fusion.5 = f32[64,256,128]{2,1,0:T(8,128)} fusion(bf16[64,128,256]{2,1,0:T(8,128)(2,1)} %gather_fusion.1, bf16[1,1,1,64,128,128]{5,4,3,2,1,0:T(8,128)(2,1)S(1)} %copy-done), kind=kOutput, calls=%fused_computation.6 | convolution fusion | flops 536870912 | bytes 14680064 | tf_op jit(solution)/shard_map/eij,ejd->eid/dot_general | solution.py:27
  182.4 9.2 %copy.12 = f32[64,256,128]{1,0,2:T(8,128)} copy(f32[64,256,128]{2,1,0:T(8,128)} %fusion.5) | data formatting | bytes 16777216 | tf_op jit(solution)/shard_map/eij,ejd->eid/dot_general | solution.py:27
  191.6 8.4 %fusion.2 = bf16[96,128,256]{2,0,1:T(8,128)(2,1)S(1)} fusion(f32[64,256,128]{1,0,2:T(8,128)} %copy.12, s32[64]{0:T(128)S(1)} %add_bitcast_fusion, pred[64]{0:T(512)(128)(4,1)S(1)} %iota_compare_fusion.1), kind=kOutput, calls=%fused_computation.4 | convolution fusion | flops 2419077120 | bytes 14680384 | tf_op jit(solution)/shard_map/se,eid->sid/dot_general | solution.py:34
  200.0 0.0 copy-start.3
  200.1 3.7 copy.10
  203.7 0.0 copy-start.1
  203.7 2.6 copy-done.1
  206.4 3.3 convolution_bitcast_fusion
  209.6 0.0 reduce-scatter.2.cloned.1.call-update
  209.7 0.0 all-gather.5.cloned.1.call-start
  209.7 42.6 %reduce-scatter.2.cloned.1.call-done = f32[256,256]{1,0:T(8,128)} async-done(((f32[2048,256]{1,0:T(8,128)}), f32[256,256]{1,0:T(8,128)}) %reduce-scatter.2.cloned.1.call-update) | async-done | bytes 262160 | tf_op jit(solution)/shard_map/reduce_scatter | solution.py:44
  252.3 1.8 multiply_convert_fusion
  254.1 0.0 all-gather.5.cloned.1.call-update
  254.1 0.0 all-reduce.3.cloned.1.call-start
  254.2 32.9 %all-gather.5.cloned.1.call-done = bf16[2048,256]{1,0:T(8,128)(2,1)} async-done(((bf16[256,256]{1,0:T(8,128)(2,1)}), bf16[2048,256]{1,0:T(8,128)(2,1)}) %all-gather.5.cloned.1.call-update) | async-done | bytes 1048592 | tf_op jit(solution)/shard_map/all_gather | solution.py:52
  287.1 6.0 fusion.7
  293.1 0.0 all-reduce.3.cloned.1.call-update
  293.1 0.0 all-reduce.5.cloned.1.call-start
  293.2 268.8 %all-reduce.3.cloned.1.call-done = f32[6,256,256]{2,1,0:T(8,128)} async-done(((f32[6,256,256]{2,1,0:T(8,128)}), f32[6,256,256]{2,1,0:T(8,128)}) %all-reduce.3.cloned.1.call-update) | async-done | bytes 1572880 | tf_op jit(solution)/shard_map/psum | solution.py:56
  562.0 0.0 all-reduce.5.cloned.1.call-update
  562.0 72.8 %all-reduce.5.cloned.1.call-done = f32[6,256,256]{2,1,0:T(8,128)} async-done(((f32[6,256,256]{2,1,0:T(8,128)}), f32[6,256,256]{2,1,0:T(8,128)}) %all-reduce.5.cloned.1.call-update) | async-done | bytes 1572880 | tf_op jit(solution)/shard_map/psum | solution.py:56
  634.9 2.7 copy.17
  (6 shorter events, 0.0 us)
Async XLA Ops:
  7.2 168.6 %copy-start = (bf16[1,1,1,64,128,128]{5,4,3,2,1,0:T(8,128)(2,1)S(1)}, bf16[1,1,1,64,128,128]{5,4,3,2,1,0:T(8,128)(2,1)}, u32[]{:S(2)}) copy-start(bf16[1,1,1,64,128,128]{5,4,3,2,1,0:T(8,128)(2,1)} %param.12) | copy-start | bytes 6291460
  7.2 157.5 %all-gather.3.cloned.1.call-start = ((), (), s32[]{:S(2)}) async-start(), calls=%async_computation.1 | async-start | bytes 8519680 | tf_op jit(solution)/shard_map/all_gather | solution.py:17
  7.9 244.4 %reduce-scatter.2.cloned.1.call-start = ((), (), s32[]{:S(2)}) async-start(), calls=%async_computation.2 | async-start | bytes 2359296 | tf_op jit(solution)/shard_map/reduce_scatter | solution.py:44
  200.0 6.3 copy-start.3
  203.7 2.7 copy-start.1
  206.4 46.0 %copy-start.2 = (bf16[256,256]{1,0:T(8,128)(2,1)S(1)}, bf16[256,256]{1,0:T(8,128)(2,1)}, u32[]{:S(2)}) copy-start(bf16[256,256]{1,0:T(8,128)(2,1)} %param.13) | copy-start | bytes 393220
  209.7 77.4 %all-gather.5.cloned.1.call-start = ((), (), s32[]{:S(2)}) async-start(), calls=%async_computation.3 | async-start | bytes 1179648 | tf_op jit(solution)/shard_map/all_gather | solution.py:52
  254.1 307.9 %all-reduce.3.cloned.1.call-start = ((), (), s32[]{:S(2)}) async-start(), calls=%async_computation.4 | async-start | bytes 3145728 | tf_op jit(solution)/shard_map/psum | solution.py:56
  293.1 341.7 %all-reduce.5.cloned.1.call-start = ((), (), s32[]{:S(2)}) async-start(), calls=%async_computation.5 | async-start | bytes 3145728 | tf_op jit(solution)/shard_map/psum | solution.py:56
Sparse Core Ops, SparseCore 0:
  10.9 153.6 all-gather.2
  209.8 42.5 reduce-scatter.1
  255.1 31.9 all-gather.4
  293.3 268.7 all-reduce.2
  564.2 70.5 all-reduce.4

commit v2 on v0

--- a/solution.py
+++ b/solution.py
@@ -14,7 +14,10 @@
     tile_rows = entry_values.shape[-1]
     features = source_feats.shape[1]
     chosen = halo_pick.reshape(-1)
-    everyone = lax.all_gather(source_feats, "dom", axis=0, tiled=True)
+    everyone = jnp.concatenate(
+        lax.all_to_all(jnp.stack([source_feats for _ in range(lax.axis_size("dom"))]), "dom", 0, 0),
+        0,
+    )
     everyone = everyone.reshape(partitions, -1, tile_rows, features)
     halo_blocks = everyone[jnp.arange(partitions, dtype=jnp.int32), chosen]
     own_rows = cotangent.shape[0]

time: 712 us -> 938 us (1.32)
  waiting for transfers between devices: 639 us -> 843 us
  starting transfers between devices: 0.16 us -> 19.3 us
    all_to_all x0 -> x1, waiting for transfers between devices: none -> 369 us  [local(): lax.all_to_all(jnp.stack([source_feats for _ in range(lax.axis_size('dom'...]
    all_gather x1 -> x0, waiting for transfers between devices: 161 us -> none  [local(): everyone = lax.all_gather(source_feats, 'dom', axis=0, tiled=True)]
    all_to_all x0 -> x1, starting transfers between devices: none -> 19.1 us  [local(): lax.all_to_all(jnp.stack([source_feats for _ in range(lax.axis_size('dom'...]
where the time goes in v2:
time: 938 us
  waiting for transfers between devices  843 us (90%)
  local copies, waits for them, and re-layouts  34.7 us (4%)
  matrix products  24.4 us (3%)
  starting transfers between devices  19.3 us (2%)
  between operations  14.5 us (2%)
    psum x1, waiting for transfers between devices, local(): grad_rel = lax.psum(weight_terms, ('dom', 'src'))  412 us
    all_to_all x1, waiting for transfers between devices, local(): lax.all_to_all(jnp.stack([source_feats for _ in range(lax.axis_size('dom'...  369 us
    all_gather x1, waiting for transfers between devices, local(): grad_rows = lax.all_gather(local_grad, ('src', 'rel'), axis=0, tiled=True)  32.6 us
    reduce_scatter x1, waiting for transfers between devices, local(): lax.psum_scatter(jnp.einsum('rtd,rde->te', relation_terms, rel_weight, pr...  29.9 us
    all_to_all x1, starting transfers between devices, local(): lax.all_to_all(jnp.stack([source_feats for _ in range(lax.axis_size('dom'...  19.1 us
  transfers between devices with their start and end apart: 4, of which 4 were waited for; matrix products, arithmetic and copies ran while one was open for 0% of the time, Pallas kernels for 0%

profile of v2, /device:TPU:2, one launch (start us, length us, event | category | flops | bytes accessed | tf_op | source)
XLA Modules:
  0.0 937.9 jit_solution(7396073094082545487)
XLA Ops:
  7.2 0.0 copy-start
  7.2 5.3 stack.2
  12.5 0.0 copy-start.4
  12.5 19.1 %all-to-all-start = ((bf16[64,256,256]{2,1,0:T(8,128)(2,1)}), bf16[64,256,256]{2,1,0:T(8,128)(2,1)}, u32[]{:S(2)}, u32[]{:S(2)}) async-start(bf16[64,256,256]{2,1,0:T(8,128)(2,1)} %stack.2), calls=%async_computation | async-start | bytes 16777216 | tf_op jit(solution)/shard_map/all_to_all | solution.py:18
  31.6 0.0 reduce-scatter.2.cloned.1.call-start
  32.3 0.0 copy-done.4
  32.4 0.0 copy-done.5
  32.4 369.0 %all-to-all-done = bf16[64,256,256]{2,1,0:T(8,128)(2,1)} async-done(((bf16[64,256,256]{2,1,0:T(8,128)(2,1)}), bf16[64,256,256]{2,1,0:T(8,128)(2,1)}, u32[]{:S(2)}, u32[]{:S(2)}) %all-to-all-start) | async-done | bytes 8388640 | tf_op jit(solution)/shard_map/all_to_all | solution.py:18
  401.4 6.2 gather_fusion
  407.5 4.9 gather_fusion.1
  412.5 0.0 copy-done
  412.5 6.7 fusion.5
  419.2 9.3 copy.12
  428.4 8.5 fusion.2
  436.9 0.0 copy-start.3
  436.9 3.7 copy.10
  440.6 0.0 copy-start.1
  440.6 2.6 copy-done.1
  443.2 0.0 copy-done.3
  443.2 3.2 convolution_bitcast_fusion
  446.5 0.0 reduce-scatter.2.cloned.1.call-update
  446.5 0.0 all-gather.2.cloned.1.call-start
  446.5 29.9 %reduce-scatter.2.cloned.1.call-done = f32[256,256]{1,0:T(8,128)} async-done(((f32[2048,256]{1,0:T(8,128)}), f32[256,256]{1,0:T(8,128)}) %reduce-scatter.2.cloned.1.call-update) | async-done | bytes 262160 | tf_op jit(solution)/shard_map/reduce_scatter | solution.py:47
  476.4 0.0 copy-done.2
  476.4 1.8 multiply_convert_fusion
  478.2 0.0 all-gather.2.cloned.1.call-update
  478.2 0.0 all-reduce.2.cloned.1.call-start
  478.3 32.6 %all-gather.2.cloned.1.call-done = bf16[2048,256]{1,0:T(8,128)(2,1)} async-done(((bf16[256,256]{1,0:T(8,128)(2,1)}), bf16[2048,256]{1,0:T(8,128)(2,1)}) %all-gather.2.cloned.1.call-update) | async-done | bytes 1048592 | tf_op jit(solution)/shard_map/all_gather | solution.py:55
  510.9 6.0 fusion.7
  516.9 0.0 all-reduce.2.cloned.1.call-update
  516.9 411.6 %all-reduce.2.cloned.1.call-done = f32[6,256,256]{2,1,0:T(8,128)} async-done(((f32[6,256,256]{2,1,0:T(8,128)}), f32[6,256,256]{2,1,0:T(8,128)}) %all-reduce.2.cloned.1.call-update) | async-done | bytes 1572880 | tf_op jit(solution)/shard_map/psum | solution.py:59
  928.6 2.7 copy.16
  (7 shorter events, 0.0 us)
Async XLA Ops:
  7.2 405.3 %copy-start = (bf16[1,1,1,64,128,128]{5,4,3,2,1,0:T(8,128)(2,1)S(1)}, bf16[1,1,1,64,128,128]{5,4,3,2,1,0:T(8,128)(2,1)}, u32[]{:S(2)}) copy-start(bf16[1,1,1,64,128,128]{5,4,3,2,1,0:T(8,128)(2,1)} %param.12) | copy-start | bytes 6291460
  12.5 19.8 %copy-start.4 = (s32[1,1,1,3,64]{4,2,3,1,0:T(1,128)S(1)}, s32[1,1,1,3,64]{4,2,3,1,0:T(1,128)}, u32[]{:S(2)}) copy-start(s32[1,1,1,3,64]{4,2,3,1,0:T(1,128)} %param.10) | copy-start | bytes 2308
  12.5 19.9 %copy-start.5 = (s32[1,1,1,64]{3,2,1,0:T(1,128)S(1)}, s32[1,1,1,64]{3,2,1,0:T(1,128)}, u32[]{:S(2)}) copy-start(s32[1,1,1,64]{3,2,1,0:T(1,128)} %param.9) | copy-start | bytes 772
  12.5 388.9 %all-to-all-start = ((bf16[64,256,256]{2,1,0:T(8,128)(2,1)}), bf16[64,256,256]{2,1,0:T(8,128)(2,1)}, u32[]{:S(2)}, u32[]{:S(2)}) async-start(bf16[64,256,256]{2,1,0:T(8,128)(2,1)} %stack.2), calls=%async_computation | async-start | bytes 16777216 | tf_op jit(solution)/shard_map/all_to_all | solution.py:18
  31.6 444.8 %reduce-scatter.2.cloned.1.call-start = ((), (), s32[]{:S(2)}) async-start(), calls=%async_computation.2 | async-start | bytes 2359296 | tf_op jit(solution)/shard_map/reduce_scatter | solution.py:47
  436.9 6.3 copy-start.3
  440.6 2.7 copy-start.1
  443.2 33.2 %copy-start.2 = (bf16[256,256]{1,0:T(8,128)(2,1)S(1)}, bf16[256,256]{1,0:T(8,128)(2,1)}, u32[]{:S(2)}) copy-start(bf16[256,256]{1,0:T(8,128)(2,1)} %param.13) | copy-start | bytes 393220
  446.5 64.4 %all-gather.2.cloned.1.call-start = ((), (), s32[]{:S(2)}) async-start(), calls=%async_computation.3 | async-start | bytes 1179648 | tf_op jit(solution)/shard_map/all_gather | solution.py:55
  478.2 450.4 %all-reduce.2.cloned.1.call-start = ((), (), s32[]{:S(2)}) async-start(), calls=%async_computation.4 | async-start | bytes 3145728 | tf_op jit(solution)/shard_map/psum | solution.py:59
Sparse Core Ops, SparseCore 0:
  446.6 29.7 reduce-scatter.1
  479.1 31.7 all-gather.1
  517.1 411.4 all-reduce.1
